TPU v7x, 32 devices: a whole 2x2x4 slice. The times are simulated.
32 devices in a mesh: comp: 8 (over y, x, core), tile: 4 (over z).
Axes of the slice: x: 2, y: 2, z: 4, core: 2. Of those that a mesh axis runs over, the one named last changes fastest.
Arguments:
- atm_state: float32 [128, 128, 512], P(None, 'comp', 'tile'), may hold values from -6 to 6
- ocean_state: float32 [48, 128, 512], P(None, 'comp', 'tile'), may hold values from -6 to 6
- atm_rate: float32 [128], replicated, may hold values from 0.02 to 0.24
- ocean_rate: float32 [48], replicated, may hold values from 0.02 to 0.24
- ocean_mask: int32 [128, 4], P('comp', 'tile'), may hold values 0 or 1
- remap_weight: bfloat16 [8, 192, 128, 128], P('comp', 'tile'), may hold values from -0.5 to 0.5
- pair_src: int32 [8, 192], P('comp', 'tile'), may hold values from 0 to 63, as said below
- pair_tgt: int32 [8, 192], P('comp', 'tile'), may hold values from 0 to 63, as said below
- pair_count: int32 [8, 4], P('comp', 'tile'), may hold values from 24 to 48, as said below
Outputs:
- atm_next: float32 [128, 128, 512], P(None, 'comp', 'tile')
- ocean_next: float32 [48, 128, 512], P(None, 'comp', 'tile')
Inputs may be any that keep to these rules, and one draw needn't show every extreme that they name: `pair_src`: entry d * 48 + j of row b names atmosphere tile e * 16 + y of band b. Among the first pair_count[b, d] entries of device d at most 13 have the same e, and every device has 13 live entries with one same e. `pair_tgt`: entry d * 48 + j of row b names ocean tile e * 16 + y of band b. Among the first pair_count[b, d] entries of device d at most 13 have the same e, and every device has 13 live entries with one same e. `pair_count`: each row b has some device with 48 live slots.
All inputs are finite; a program needn't handle non-finite values. No bound on the sum of `ocean_mask` on one device may be relied on, other than what follows from the above.
Results may differ from a plain program's by a relative error of at most 0.002.
Values may be sent and summed in bfloat16 or wider, within the bound.
No kernel may reach another device: no remote copies, remote signals or barrier semaphores. Data moves between devices by JAX's collectives and lax.ppermute only.
A program may use at most 64 MiB of HBM per device.

v0:
```python
import jax
import jax.numpy as jnp
from jax import lax
from jax.sharding import PartitionSpec as P

SURF = 8


def padded_2(block, sides, width):
    for axis, dim in sides:
        count = lax.axis_size(axis)
        forward = [(i, i + 1) for i in range(count - 1)]
        forward.append((count - 1, 0))
        backward = [(target, source) for source, target in forward]
        low = lax.ppermute(
            lax.slice_in_dim(block, block.shape[dim] - width, None, axis=dim), axis, forward
        )
        high = lax.ppermute(lax.slice_in_dim(block, 0, width, axis=dim), axis, backward)
        block = jnp.concatenate([low, block, high], axis=dim)
    return block


def relax(padded, spread):
    center = padded[:, 1:-1, 1:-1]
    beside_all = (
        padded[:, 2:, 1:-1] + padded[:, :-2, 1:-1] + padded[:, 1:-1, 2:] + padded[:, 1:-1, :-2]
    )
    return center + spread[:, None, None] * (beside_all - 4.0 * center)


def ghosts(padded, width):
    row_total = padded.shape[1]
    row_index = jnp.arange(row_total)
    position = lax.axis_index("comp")
    at_first = jnp.logical_and(row_index < width, position == 0)
    at_last = jnp.logical_and(row_index >= row_total - width, position == lax.axis_size("comp") - 1)
    retain = jnp.logical_not(jnp.logical_or(at_first, at_last)).astype(jnp.float32)
    return padded * retain[None, :, None]


def shards(
    atm_state,
    ocean_state,
    atm_rate,
    ocean_rate,
    ocean_mask,
    remap_weight,
    pair_src,
    pair_tgt,
    pair_count,
):
    atm_rows = atm_state.shape[1]
    ocean_rows = ocean_state.shape[1]
    cell_total = atm_state.shape[2]
    pair_total = pair_src.shape[1]
    wet_rows = ocean_mask[:, 0].astype(jnp.float32)
    atm_source = atm_state[:SURF].astype(jnp.bfloat16)
    ocean_source = (ocean_state[:SURF] * wet_rows[None, :, None]).astype(jnp.bfloat16)
    atm_band, ocean_band = (
        lax.all_gather(atm_source, "tile", axis=1, tiled=True),
        lax.all_gather(ocean_source, "tile", axis=1, tiled=True),
    )
    anchor = pair_src[0]
    target = pair_tgt[0]
    active = jnp.arange(pair_total) < pair_count[0, 0]
    active_float = active.astype(jnp.float32)[:, None, None]
    weights = remap_weight[0]
    forward = (
        jnp.einsum(
            "fpt,pts->pfs",
            jnp.take(atm_band, anchor, axis=1),
            weights,
            preferred_element_type=jnp.float32,
        )
        * active_float
    )
    reverse = (
        jnp.einsum(
            "fps,pts->pft",
            jnp.take(ocean_band, target, axis=1),
            weights,
            preferred_element_type=jnp.float32,
        )
        * active_float
    )
    band_rows = atm_rows + ocean_rows
    ahead_codes = jnp.where(
        active, target // ocean_rows * band_rows + atm_rows + target % ocean_rows, -1
    )
    back_codes = jnp.where(active, anchor // atm_rows * band_rows + anchor % atm_rows, -1)
    ahead_flat = forward.reshape(pair_total, -1)
    back_flat = reverse.reshape(pair_total, -1)
    row_codes = jnp.arange(band_rows * lax.axis_size("tile"))
    ahead_hot = (row_codes[:, None] == ahead_codes[None, :]).astype(jnp.float32)
    back_hot = (row_codes[:, None] == back_codes[None, :]).astype(jnp.float32)
    summed = lax.psum_scatter(
        jnp.dot(
            ahead_hot,
            ahead_flat,
            precision=lax.Precision.HIGHEST,
            preferred_element_type=jnp.float32,
        )
        + jnp.dot(
            back_hot, back_flat, precision=lax.Precision.HIGHEST, preferred_element_type=jnp.float32
        ),
        "tile",
        scatter_dimension=0,
        tiled=True,
    )
    atm_force = summed[:atm_rows].reshape(atm_rows, SURF, cell_total)
    ocean_force = summed[atm_rows:].reshape(ocean_rows, SURF, cell_total)
    atm_padded = ghosts(padded_2(atm_state, (("comp", 1), ("tile", 2)), 2), 2)
    atm_stepped = relax(ghosts(relax(atm_padded, atm_rate), 1), atm_rate)
    ocean_padded = ghosts(padded_2(ocean_state, (("comp", 1), ("tile", 2)), 2), 2)
    ocean_stepped = relax(ghosts(relax(ocean_padded, ocean_rate), 1), ocean_rate)
    atm_next = atm_stepped.at[:SURF].add(jnp.transpose(atm_force, (1, 0, 2)))
    ocean_next = ocean_stepped.at[:SURF].add(
        jnp.transpose(ocean_force, (1, 0, 2)) * wet_rows[None, :, None]
    )
    return (atm_next, ocean_next)


def solution(mesh):
    return jax.shard_map(
        shards,
        mesh=mesh,
        in_specs=(
            P(None, "comp", "tile"),
            P(None, "comp", "tile"),
            P(),
            P(),
            P("comp", "tile"),
            P("comp", "tile", None, None),
            P("comp", "tile"),
            P("comp", "tile"),
            P("comp", "tile"),
        ),
        out_specs=(P(None, "comp", "tile"), P(None, "comp", "tile")),
        check_vma=False,
    )
```

profile of v0, /device:TPU:0, one launch (start us, length us, event | category | flops | bytes accessed | tf_op | source)
XLA Modules:
  0.0 102.0 jit_solution(3758282511293976926)
XLA Ops:
  7.3 2.0 %copy.67 = f32[128,16,128]{0,1,2:T(8,128)S(1)} copy(f32[128,16,128]{2,1,0:T(8,128)} %param.15) | data formatting | bytes 2097152 | tf_op args[0]
  10.6 2.9 %collective-permute-start.1 = (f32[128,2,128]{0,1,2:T(2,128)}, f32[128,2,128]{0,1,2:T(2,128)}, u32[]{:S(2)}, u32[]{:S(2)}) collective-permute-start(f32[128,2,128]{0,1,2:T(2,128)} %get-tuple-element.38), channel_id=1, source_target_pairs={{4,0},{8,4},{12,8},{16,12},{20,16},{24,20},{28,24},{0,28},{5,1},{9... | collective-permute-start | bytes 393224 | tf_op jit(solution)/shard_map/ppermute | solution.py:18
  15.0 14.4 %all_gather.6 = bf16[8,64,128]{2,0,1:T(8,128)(2,1)S(1)} all-gather(bf16[8,16,128]{2,0,1:T(8,128)(2,1)S(1)} %copy.100), channel_id=1, replica_groups=mesh['comp'=8,'tile'=4] {'tile'}, dimensions={1}, use_global_device_ids=true | all-gather | bytes 163840 | tf_op jit(solution)/shard_map/all_gather | solution.py:60
  30.9 14.3 %all_gather.7 = bf16[8,64,128]{2,0,1:T(8,128)(2,1)} all-gather(bf16[8,16,128]{2,0,1:T(8,128)(2,1)S(1)} %fusion.36), channel_id=1, replica_groups=mesh['comp'=8,'tile'=4] {'tile'}, dimensions={1}, use_global_device_ids=true | all-gather | bytes 163840 | tf_op jit(solution)/shard_map/all_gather | solution.py:61
  47.4 2.1 %gather_fusion.1 = bf16[48,8,128]{2,1,0:T(8,128)(2,1)} fusion(bf16[8,64,128]{2,0,1:T(8,128)(2,1)} %all_gather.7, s32[1024]{0:T(1024)S(1)} %pad_clamp_fusion), kind=kCustom, calls=%fused_computation.1.clone | custom fusion | bytes 196800 | tf_op jit(solution)/shard_map/jit(_take)/gather | solution.py:80
  49.6 1.8 %fusion.11 = f32[48,8,128]{2,1,0:T(8,128)S(1)} fusion(bf16[1,48,128,128]{3,2,1,0:T(8,128)(2,1)S(1)} %copy-done, bf16[48,8,128]{2,1,0:T(8,128)(2,1)} %gather_fusion.1, f32[48]{0:T(128)S(1)} %compare_convert_fusion, pred[48]{0:T(512)(128)(4,1)S(1)} %compare_and_fusion), kind=kOutput, calls=%fused_computation.17 | convolution fusion | flops 12681216 | bytes 1868016 | tf_op jit(solution)/shard_map/fps,pts->pft/dot_general | solution.py:78
  51.4 1.9 %convolution_add_fusion = f32[128,1024]{1,0:T(8,128)} fusion(f32[128,1024]{1,0:T(8,128)S(1)} %fusion.26, f32[6,8,8,128]{3,2,1,0:T(8,128)S(1)} %bitcast.52, s32[48]{0:T(128)} %fusion.44), kind=kOutput, calls=%fused_computation.15 | convolution fusion | flops 75634688 | bytes 1245376 | tf_op jit(solution)/shard_map/dot_general | solution.py:103
  53.3 1.4 %fusion.50 = (f32[48,2,128]{2,0,1:T(8,128)}, f32[48,2,128]{2,0,1:T(8,128)S(1)}) fusion(f32[48,16,128]{2,0,1:T(8,128)} %copy-done.2), kind=kLoop, calls=%fused_computation.98 | loop fusion | bytes 196608 | tf_op jit(solution)/shard_map/slice | solution.py:18
  54.8 2.6 %collective-permute-start.5 = (f32[48,2,128]{2,0,1:T(8,128)}, f32[48,2,128]{2,0,1:T(8,128)}, u32[]{:S(2)}, u32[]{:S(2)}) collective-permute-start(f32[48,2,128]{2,0,1:T(8,128)} %get-tuple-element.41), channel_id=1, source_target_pairs={{4,0},{8,4},{12,8},{16,12},{20,16},{24,20},{28,24},{0,28},{5,1},{9... | collective-permute-start | bytes 147464 | tf_op jit(solution)/shard_map/ppermute | solution.py:18
  57.4 1.9 %collective-permute-done.4 = f32[48,2,128]{2,0,1:T(8,128)} collective-permute-done((f32[48,2,128]{2,0,1:T(8,128)S(1)}, f32[48,2,128]{2,0,1:T(8,128)}, u32[]{:S(2)}, u32[]{:S(2)}) %collective-permute-start.4) | collective-permute-done | bytes 49184 | tf_op jit(solution)/shard_map/ppermute | solution.py:15
  61.0 1.1 %fusion.49 = (f32[48,20,2]{2,0,1:T(8,128)}, f32[48,20,2]{2,0,1:T(8,128)}) fusion(f32[48,20,128]{2,0,1:T(8,128)S(1)} %constant_dynamic-update-slice_fusion), kind=kLoop, calls=%fused_computation.97 | loop fusion | bytes 30720 | tf_op jit(solution)/shard_map/slice | solution.py:16
  62.1 1.3 %copy.79 = f32[48,20,2]{0,1,2:T(8,128)S(1)} copy(f32[48,20,2]{2,0,1:T(8,128)} %get-tuple-element.39) | data formatting | bytes 15360 | tf_op jit(solution)/shard_map/slice | solution.py:16
  63.3 1.5 %collective-permute-start.6 = (f32[48,20,2]{0,1,2:T(8,128)S(1)}, f32[48,20,2]{0,1,2:T(8,128)S(1)}, u32[]{:S(2)}, u32[]{:S(2)}) collective-permute-start(f32[48,20,2]{0,1,2:T(8,128)S(1)} %copy.79), channel_id=1, source_target_pairs={{0,1},{1,2},{2,3},{3,0},{4,5},{5,6},{6,7},{7,4},{8,9},{9,10},{10,1... | collective-permute-start | bytes 23048 | tf_op jit(solution)/shard_map/ppermute | solution.py:15
  64.9 1.3 %copy.80 = f32[48,20,2]{0,1,2:T(8,128)S(1)} copy(f32[48,20,2]{2,0,1:T(8,128)} %get-tuple-element.40) | data formatting | bytes 15360 | tf_op jit(solution)/shard_map/slice | solution.py:18
  66.2 2.4 %collective-permute-start.7 = (f32[48,20,2]{0,1,2:T(8,128)S(1)}, f32[48,20,2]{0,1,2:T(8,128)S(1)}, u32[]{:S(2)}, u32[]{:S(2)}) collective-permute-start(f32[48,20,2]{0,1,2:T(8,128)S(1)} %copy.80), channel_id=1, source_target_pairs={{1,0},{2,1},{3,2},{0,3},{5,4},{6,5},{7,6},{4,7},{9,8},{10,9},{11,1... | collective-permute-start | bytes 23048 | tf_op jit(solution)/shard_map/ppermute | solution.py:18
  69.4 1.0 %copy.81 = f32[48,20,2]{2,0,1:T(8,128)} copy(f32[48,20,2]{0,1,2:T(8,128)S(1)} %collective-permute-done.6) | data formatting | bytes 15360 | tf_op jit(solution)/shard_map/ppermute | solution.py:15
  71.5 1.6 %maximum_multiply_fusion.1 = f32[48,20,132]{2,0,1:T(8,128)S(1)} fusion(f32[48,20,2]{2,0,1:T(8,128)} %copy.82, f32[48,20,128]{2,0,1:T(8,128)S(1)} %constant_dynamic-update-slice_fusion, f32[48,20,2]{2,0,1:T(8,128)} %copy.81, f32[20]{0:T(128)S(1)} %not_convert_fusion.1), kind=kLoop, calls=%fused_computation.25 | loop fusion | flops 380160 | bytes 1013840 | tf_op jit(solution)/shard_map/mul | solution.py:38
  74.2 1.2 %pad_maximum_fusion = f32[128,20,128]{0,1,2:T(8,128)S(1)} fusion(f32[128,2,128]{0,1,2:T(2,128)} %collective-permute-done.1, f32[128,16,128]{0,1,2:T(8,128)S(1)} %copy.67, f32[128,2,128]{0,1,2:T(2,128)} %collective-permute-done), kind=kLoop, calls=%fused_computation.2 | loop fusion | flops 655360 | bytes 2621440 | tf_op jit(solution)/shard_map/concatenate | solution.py:19
  75.4 1.3 %collective-permute-start.2 = (f32[128,20,2]{0,1,2:T(8,128)S(1)}, f32[128,20,2]{0,1,2:T(8,128)S(1)}, u32[]{:S(2)}, u32[]{:S(2)}) collective-permute-start(f32[128,20,2]{0,1,2:T(8,128)S(1)} %get-tuple-element.35), channel_id=1, source_target_pairs={{0,1},{1,2},{2,3},{3,0},{4,5},{5,6},{6,7},{7,4},{8,9},{9,10},{10,1... | collective-permute-start | bytes 61448 | tf_op jit(solution)/shard_map/ppermute | solution.py:15
  76.7 3.1 %collective-permute-start.3 = (f32[128,20,2]{0,1,2:T(8,128)S(1)}, f32[128,20,2]{0,1,2:T(8,128)S(1)}, u32[]{:S(2)}, u32[]{:S(2)}) collective-permute-start(f32[128,20,2]{0,1,2:T(8,128)S(1)} %get-tuple-element.36), channel_id=1, source_target_pairs={{1,0},{2,1},{3,2},{0,3},{5,4},{6,5},{7,6},{4,7},{9,8},{10,9},{11,1... | collective-permute-start | bytes 61448 | tf_op jit(solution)/shard_map/ppermute | solution.py:18
  84.0 1.3 %copy.75 = f32[16,8,128]{1,2,0:T(8,128)} copy(f32[16,8,128]{2,1,0:T(8,128)S(1)} %bitcast.54) | data formatting | bytes 131072 | tf_op jit(solution)/shard_map/reshape | solution.py:110
  85.4 2.3 %slice_add_fusion.3 = f32[8,16,128]{0,2,1:T(8,128)} fusion(f32[128,16,128]{0,2,1:T(8,128)S(1)} %fusion.16, f32[16,8,128]{1,2,0:T(8,128)} %copy.75), kind=kLoop, calls=%fused_computation.18 | loop fusion | flops 16384 | bytes 196608 | tf_op jit(solution)/shard_map/add | solution.py:116
  87.7 5.1 %scatter-add.6 = f32[128,16,128]{0,2,1:T(8,128)S(1)} dynamic-update-slice(f32[128,16,128]{0,2,1:T(8,128)S(1)} %fusion.16, f32[8,16,128]{0,2,1:T(8,128)} %slice_add_fusion.3, s32[]{:T(128)} %constant.113.clone.1, s32[]{:T(128)} %constant.113.clone.1, s32[]{:T(128)} %constant.113.clone.1) | dynamic-update-slice | bytes 131076 | tf_op jit(solution)/shard_map/scatter-add | solution.py:116
  92.8 1.4 %copy.83 = f32[128,16,128]{2,1,0:T(8,128)} copy(f32[128,16,128]{0,2,1:T(8,128)S(1)} %scatter-add.6) | data formatting | bytes 2097152
  (68 shorter events, 15.8 us)
Async XLA Ops:
  7.2 39.2 %copy-start = (bf16[1,48,128,128]{3,2,1,0:T(8,128)(2,1)S(1)}, bf16[1,48,128,128]{3,2,1,0:T(8,128)(2,1)}, u32[]{:S(2)}) copy-start(bf16[1,48,128,128]{3,2,1,0:T(8,128)(2,1)} %param.20) | copy-start | bytes 4718596
  7.2 7.1 %copy-start.8 = (s32[1,48]{1,0:T(1,128)S(1)}, s32[1,48]{1,0:T(1,128)}, u32[]{:S(2)}) copy-start(s32[1,48]{1,0:T(1,128)} %param.21) | copy-start | bytes 580
  7.2 7.1 %copy-start.6 = (s32[1,48]{1,0:T(1,128)S(1)}, s32[1,48]{1,0:T(1,128)}, u32[]{:S(2)}) copy-start(s32[1,48]{1,0:T(1,128)} %param.22) | copy-start | bytes 580
  7.2 22.7 %copy-start.1 = (f32[48,16,128]{2,1,0:T(8,128)S(1)}, f32[48,16,128]{2,1,0:T(8,128)}, u32[]{:S(2)}) copy-start(f32[48,16,128]{2,1,0:T(8,128)} %param.16) | copy-start | bytes 1179652
  7.2 22.9 %copy-start.7 = (s32[16,1]{0,1:T(1,128)S(1)}, s32[16,1]{0,1:T(1,128)}, u32[]{:S(2)}) copy-start(s32[16,1]{0,1:T(1,128)} %param.19) | copy-start | bytes 196
  7.2 75.9 %reduce-scatter.2.cloned.1.call-start = ((), (), s32[]{:S(2)}) async-start(), calls=%async_computation.1 | async-start | bytes 655360 | tf_op jit(solution)/shard_map/reduce_scatter | solution.py:96
  10.1 64.1 %collective-permute-start = (f32[128,2,128]{0,1,2:T(2,128)}, f32[128,2,128]{0,1,2:T(2,128)}, u32[]{:S(2)}, u32[]{:S(2)}) collective-permute-start(f32[128,2,128]{0,1,2:T(2,128)} %get-tuple-element.37), channel_id=1, source_target_pairs={{0,4},{4,8},{8,12},{12,16},{16,20},{20,24},{24,28},{28,0},{1,5},{5... | collective-permute-start | bytes 393224 | tf_op jit(solution)/shard_map/ppermute | solution.py:15
  10.6 63.6 %collective-permute-start.1 = (f32[128,2,128]{0,1,2:T(2,128)}, f32[128,2,128]{0,1,2:T(2,128)}, u32[]{:S(2)}, u32[]{:S(2)}) collective-permute-start(f32[128,2,128]{0,1,2:T(2,128)} %get-tuple-element.38), channel_id=1, source_target_pairs={{4,0},{8,4},{12,8},{16,12},{20,16},{24,20},{28,24},{0,28},{5,1},{9... | collective-permute-start | bytes 393224 | tf_op jit(solution)/shard_map/ppermute | solution.py:18
  30.1 0.7 copy-start.2
  46.4 0.6 copy-start.5
  54.8 4.5 %collective-permute-start.4 = (f32[48,2,128]{2,0,1:T(8,128)S(1)}, f32[48,2,128]{2,0,1:T(8,128)}, u32[]{:S(2)}, u32[]{:S(2)}) collective-permute-start(f32[48,2,128]{2,0,1:T(8,128)S(1)} %get-tuple-element.42), channel_id=1, source_target_pairs={{0,4},{4,8},{8,12},{12,16},{16,20},{20,24},{24,28},{28,0},{1,5},{5... | collective-permute-start | bytes 147464 | tf_op jit(solution)/shard_map/ppermute | solution.py:15
  54.8 5.4 %collective-permute-start.5 = (f32[48,2,128]{2,0,1:T(8,128)}, f32[48,2,128]{2,0,1:T(8,128)}, u32[]{:S(2)}, u32[]{:S(2)}) collective-permute-start(f32[48,2,128]{2,0,1:T(8,128)} %get-tuple-element.41), channel_id=1, source_target_pairs={{4,0},{8,4},{12,8},{16,12},{20,16},{24,20},{28,24},{0,28},{5,1},{9... | collective-permute-start | bytes 147464 | tf_op jit(solution)/shard_map/ppermute | solution.py:18
  63.3 6.0 %collective-permute-start.6 = (f32[48,20,2]{0,1,2:T(8,128)S(1)}, f32[48,20,2]{0,1,2:T(8,128)S(1)}, u32[]{:S(2)}, u32[]{:S(2)}) collective-permute-start(f32[48,20,2]{0,1,2:T(8,128)S(1)} %copy.79), channel_id=1, source_target_pairs={{0,1},{1,2},{2,3},{3,0},{4,5},{5,6},{6,7},{7,4},{8,9},{9,10},{10,1... | collective-permute-start | bytes 23048 | tf_op jit(solution)/shard_map/ppermute | solution.py:15
  66.2 4.3 %collective-permute-start.7 = (f32[48,20,2]{0,1,2:T(8,128)S(1)}, f32[48,20,2]{0,1,2:T(8,128)S(1)}, u32[]{:S(2)}, u32[]{:S(2)}) collective-permute-start(f32[48,20,2]{0,1,2:T(8,128)S(1)} %copy.80), channel_id=1, source_target_pairs={{1,0},{2,1},{3,2},{0,3},{5,4},{6,5},{7,6},{4,7},{9,8},{10,9},{11,1... | collective-permute-start | bytes 23048 | tf_op jit(solution)/shard_map/ppermute | solution.py:18
  70.4 2.7 %copy-start.3 = (f32[48]{0:T(128)S(1)}, f32[48]{0:T(128)}, u32[]{:S(2)}) copy-start(f32[48]{0:T(128)} %param.18) | copy-start | bytes 580
  75.4 6.1 %collective-permute-start.2 = (f32[128,20,2]{0,1,2:T(8,128)S(1)}, f32[128,20,2]{0,1,2:T(8,128)S(1)}, u32[]{:S(2)}, u32[]{:S(2)}) collective-permute-start(f32[128,20,2]{0,1,2:T(8,128)S(1)} %get-tuple-element.35), channel_id=1, source_target_pairs={{0,1},{1,2},{2,3},{3,0},{4,5},{5,6},{6,7},{7,4},{8,9},{9,10},{10,1... | collective-permute-start | bytes 61448 | tf_op jit(solution)/shard_map/ppermute | solution.py:15
  76.7 4.9 %collective-permute-start.3 = (f32[128,20,2]{0,1,2:T(8,128)S(1)}, f32[128,20,2]{0,1,2:T(8,128)S(1)}, u32[]{:S(2)}, u32[]{:S(2)}) collective-permute-start(f32[128,20,2]{0,1,2:T(8,128)S(1)} %get-tuple-element.36), channel_id=1, source_target_pairs={{1,0},{2,1},{3,2},{0,3},{5,4},{6,5},{7,6},{4,7},{9,8},{10,9},{11,1... | collective-permute-start | bytes 61448 | tf_op jit(solution)/shard_map/ppermute | solution.py:18
  81.6 0.7 copy-start.4
Sparse Core Ops, SparseCore 0:
  53.4 22.3 reduce-scatter.1
where the time goes:
time: 103 us; the launch traced here: 102 us
  blocking collectives  28.6 us (28%)
  local copies, waits for them, and re-layouts  26.5 us (26%)
  between operations  15 us (15%)
  starting transfers between devices  14.4 us (14%)
  other arithmetic  9.11 us (9%)
  matrix products  4.66 us (5%)
  waiting for transfers between devices  3.77 us (4%)
    all_gather x1, blocking collectives, shards(): lax.all_gather(atm_source, 'tile', axis=1, tiled=True)  14.4 us
    all_gather x1, blocking collectives, shards(): lax.all_gather(ocean_source, 'tile', axis=1, tiled=True)  14.3 us
    ppermute x4, starting transfers between devices, padded_2(): lax.ppermute(lax.slice_in_dim(block, 0, width, axis=dim), axis, backward)  11 us
    unnamed x28, local copies, waits for them, and re-layouts  7.44 us
    scatter-add x1, local copies, waits for them, and re-layouts, shards(): atm_next = atm_stepped.at[:SURF].add(jnp.transpose(atm_force, (1, 0, 2)))  5.1 us
    ppermute x4, waiting for transfers between devices, padded_2(): lax.ppermute(lax.slice_in_dim(block, block.shape[dim] - width, None, axis...  3.67 us
    mul x4, other arithmetic, ghosts(): return padded * retain[None, :, None]  3.33 us
    ppermute x4, starting transfers between devices, padded_2(): lax.ppermute(lax.slice_in_dim(block, block.shape[dim] - width, None, axis...  3.33 us
  transfers between devices with their start and end apart: 9, of which 4 were waited for; matrix products, arithmetic and copies ran while one was open for 24% of the time, Pallas kernels for 0%

commit v1 on v0

--- a/solution.py
+++ b/solution.py
@@ -1,9 +1,42 @@
+import functools
 import jax
 import jax.numpy as jnp
 from jax import lax
 from jax.sharding import PartitionSpec as P
 
 SURF = 8
+
+
+def _check_run(in_array, axis_k):
+    carry_in = lax.axis_size("tile")
+    part_now = lax.axis_index("tile")
+    z1, passed, heard = (carry_in, part_now, in_array.shape[axis_k])
+    tray = []
+    for idx, k in enumerate(in_array.shape):
+        tray.append(k * z1 if idx == axis_k else k)
+    block_now = jnp.zeros(tray, in_array.dtype)
+    spare = lax.dynamic_update_slice_in_dim(block_now, in_array, passed * heard, axis=axis_k)
+    outer = formed = in_array
+    for ix in range(1, z1 // 2 + 1):
+        panels = []
+        for idx in range(z1):
+            panels.append((idx, (idx + 1) % z1))
+        outer = lax.ppermute(outer, "tile", panels)
+        spare = lax.dynamic_update_slice_in_dim(
+            spare, outer, (passed - ix) % z1 * heard, axis=axis_k
+        )
+        if 2 * ix < z1:
+            buffers = []
+            for idx in range(z1):
+                buffers.append((idx, (idx - 1) % z1))
+            formed = lax.ppermute(formed, "tile", buffers)
+            spare = lax.dynamic_update_slice_in_dim(
+                spare, formed, (passed + ix) % z1 * heard, axis=axis_k
+            )
+    return spare
+
+
+raise_the_cube = functools.partial(_check_run, axis_k=1)
 
 
 def padded_2(block, sides, width):
@@ -57,7 +90,7 @@
     atm_source = atm_state[:SURF].astype(jnp.bfloat16)
     ocean_source = (ocean_state[:SURF] * wet_rows[None, :, None]).astype(jnp.bfloat16)
     atm_band, ocean_band = (
-        lax.all_gather(atm_source, "tile", axis=1, tiled=True),
+        raise_the_cube(atm_source),
         lax.all_gather(ocean_source, "tile", axis=1, tiled=True),
     )
     anchor = pair_src[0]

time: 103 us -> 106 us (1.029)
  blocking collectives: 28.6 us -> 13.4 us
  waiting for transfers between devices: 3.77 us -> 18.5 us
  other arithmetic: 9.11 us -> 12.7 us
  local copies, waits for them, and re-layouts: 26.5 us -> 28.8 us
  starting transfers between devices: 14.4 us -> 12.4 us
    all_gather x1 -> x0, blocking collectives: 14.4 us -> none  [shards(): lax.all_gather(atm_source, 'tile', axis=1, tiled=True)]
    reduce_scatter x1, waiting for transfers between devices: 0.02 us -> 11.9 us  [shards(): lax.psum_scatter(jnp.dot(ahead_hot, ahead_flat, precision=lax.Precision.H...]
    ppermute x4, starting transfers between devices: 11 us -> 5.57 us  [padded_2(): lax.ppermute(lax.slice_in_dim(block, 0, width, axis=dim), axis, backward)]
    ppermute x0 -> x3, starting transfers between devices: none -> 5.19 us  [the longest x2 3.1 us: _check_run(): outer = lax.ppermute(outer, 'tile', panels)]
    dynamic_update_slice x0 -> x4, local copies, waits for them, and re-layouts: none -> 4.72 us  [the longest x2 2.73 us: _check_run(): lax.dynamic_update_slice_in_dim(spare, outer, (passed - ix) % z1 * heard,...]
    ppermute x4, waiting for transfers between devices: 3.67 us -> 5.68 us  [padded_2(): lax.ppermute(lax.slice_in_dim(block, block.shape[dim] - width, None, axis...]
    ppermute x4, starting transfers between devices: 3.33 us -> 1.65 us  [padded_2(): lax.ppermute(lax.slice_in_dim(block, block.shape[dim] - width, None, axis...]
    gather x1, local copies, waits for them, and re-layouts: 0.61 us -> 2.27 us  [shards(): jnp.take(atm_band, anchor, axis=1)]
  transfers between devices with their start and end apart: 9 -> 12, of which waited for: 4 -> 5; matrix products, arithmetic and copies ran while one was open for 24% -> 30% of each run, Pallas kernels for 0% -> 0%
where the time goes in v1:
time: 106 us
  local copies, waits for them, and re-layouts  28.8 us (27%)
  waiting for transfers between devices  18.5 us (17%)
  between operations  15 us (14%)
  blocking collectives  13.4 us (13%)
  other arithmetic  12.7 us (12%)
  starting transfers between devices  12.4 us (12%)
  matrix products  4.72 us (4%)
    all_gather x1, blocking collectives, shards(): lax.all_gather(ocean_source, 'tile', axis=1, tiled=True)  13.4 us
    reduce_scatter x1, waiting for transfers between devices, shards(): lax.psum_scatter(jnp.dot(ahead_hot, ahead_flat, precision=lax.Precision.H...  11.9 us
    unnamed x45, local copies, waits for them, and re-layouts  5.8 us
    ppermute x4, waiting for transfers between devices, padded_2(): lax.ppermute(lax.slice_in_dim(block, block.shape[dim] - width, None, axis...  5.68 us
    ppermute x4, starting transfers between devices, padded_2(): lax.ppermute(lax.slice_in_dim(block, 0, width, axis=dim), axis, backward)  5.57 us
    scatter-add x1, local copies, waits for them, and re-layouts, shards(): atm_next = atm_stepped.at[:SURF].add(jnp.transpose(atm_force, (1, 0, 2)))  5.1 us
    mul x4, other arithmetic, ghosts(): return padded * retain[None, :, None]  3.34 us
    slice x4, local copies, waits for them, and re-layouts, padded_2(): lax.slice_in_dim(block, block.shape[dim] - width, None, axis=dim)  3.15 us
  transfers between devices with their start and end apart: 12, of which 5 were waited for; matrix products, arithmetic and copies ran while one was open for 30% of the time, Pallas kernels for 0%

profile of v1, /device:TPU:0, one launch (start us, length us, event | category | flops | bytes accessed | tf_op | source)
XLA Modules:
  0.0 105.6 jit_solution(17020898010968369525)
XLA Ops:
  9.5 3.1 %collective-permute-start.4 = (bf16[8,16,128]{2,0,1:T(8,128)(2,1)}, bf16[8,16,128]{2,0,1:T(8,128)(2,1)}, u32[]{:S(2)}, u32[]{:S(2)}) collective-permute-start(bf16[8,16,128]{2,0,1:T(8,128)(2,1)} %get-tuple-element.36), channel_id=1, source_target_pairs={{0,1},{1,2},{2,3},{3,0},{4,5},{5,6},{6,7},{7,4},{8,9},{9,10},{10,1... | collective-permute-start | bytes 98312 | tf_op jit(solution)/shard_map/ppermute | solution.py:24
  12.6 2.1 %collective-permute-start.5 = (bf16[8,16,128]{2,0,1:T(8,128)(2,1)}, bf16[8,16,128]{2,0,1:T(8,128)(2,1)}, u32[]{:S(2)}, u32[]{:S(2)}) collective-permute-start(bf16[8,16,128]{2,0,1:T(8,128)(2,1)} %get-tuple-element.36), channel_id=1, source_target_pairs={{0,3},{1,0},{2,1},{3,2},{4,7},{5,4},{6,5},{7,6},{8,11},{9,8},{10,9... | collective-permute-start | bytes 98312 | tf_op jit(solution)/shard_map/ppermute | solution.py:32
  14.7 1.8 %copy.66 = f32[128,16,128]{0,1,2:T(8,128)S(1)} copy(f32[128,16,128]{2,1,0:T(8,128)} %param.15) | data formatting | bytes 2097152 | tf_op args[0]
  17.3 1.6 %collective-permute-start.1 = (f32[128,2,128]{0,1,2:T(2,128)}, f32[128,2,128]{0,1,2:T(2,128)}, u32[]{:S(2)}, u32[]{:S(2)}) collective-permute-start(f32[128,2,128]{0,1,2:T(2,128)} %get-tuple-element.40), channel_id=1, source_target_pairs={{4,0},{8,4},{12,8},{16,12},{20,16},{24,20},{28,24},{0,28},{5,1},{9... | collective-permute-start | bytes 393224 | tf_op jit(solution)/shard_map/ppermute | solution.py:51
  22.8 13.4 %all_gather.3 = bf16[8,64,128]{2,0,1:T(8,128)(2,1)S(1)} all-gather(bf16[8,16,128]{2,0,1:T(8,128)(2,1)S(1)} %fusion.36), channel_id=1, replica_groups=mesh['comp'=8,'tile'=4] {'tile'}, dimensions={1}, use_global_device_ids=true | all-gather | bytes 163840 | tf_op jit(solution)/shard_map/all_gather | solution.py:94
  36.2 1.2 %fusion.44 = s32[48]{0:T(128)} fusion(s32[1,48]{1,0:T(1,128)} %param.21, s32[]{:T(128)} %bitcast.51), kind=kLoop, calls=%fused_computation.95 | loop fusion | flops 1104 | bytes 388 | tf_op jit(solution)/shard_map/eq | solution.py:128
  38.6 1.6 %fusion.11 = f32[48,8,128]{2,1,0:T(8,128)} fusion(bf16[1,48,128,128]{3,2,1,0:T(8,128)(2,1)S(1)} %copy-done, bf16[48,8,128]{2,1,0:T(8,128)(2,1)S(1)} %gather_fusion.1, f32[48]{0:T(128)S(1)} %compare_convert_fusion, pred[48]{0:T(512)(128)(4,1)S(1)} %compare_and_fusion), kind=kOutput, calls=%fused_computation.17 | convolution fusion | flops 12681216 | bytes 1868016 | tf_op jit(solution)/shard_map/fps,pts->pft/dot_general | solution.py:111
  40.8 1.4 %constant_dynamic-update-slice_fusion.5 = bf16[8,64,128]{2,0,1:T(8,128)(2,1)} fusion(bf16[8,64,128]{2,0,1:T(8,128)(2,1)} %get-tuple-element.35, bf16[8,16,128]{2,0,1:T(8,128)(2,1)} %collective-permute-done.4, s32[]{:T(128)S(6)} %select_n.69), kind=kLoop, calls=%fused_computation.82 | loop fusion | bytes 65540 | tf_op jit(solution)/shard_map/dynamic_update_slice | solution.py:25
  44.0 1.3 %copy.79 = f32[48,20,2]{0,1,2:T(8,128)S(1)} copy(f32[48,20,2]{2,0,1:T(8,128)} %get-tuple-element.42) | data formatting | bytes 15360 | tf_op jit(solution)/shard_map/slice | solution.py:51
  45.2 3.3 %collective-permute-start.10 = (f32[48,20,2]{0,1,2:T(8,128)S(1)}, f32[48,20,2]{0,1,2:T(8,128)S(1)}, u32[]{:S(2)}, u32[]{:S(2)}) collective-permute-start(f32[48,20,2]{0,1,2:T(8,128)S(1)} %copy.79), channel_id=1, source_target_pairs={{1,0},{2,1},{3,2},{0,3},{5,4},{6,5},{7,6},{4,7},{9,8},{10,9},{11,1... | collective-permute-start | bytes 23048 | tf_op jit(solution)/shard_map/ppermute | solution.py:51
  48.6 1.3 %copy.78 = f32[48,20,2]{0,1,2:T(8,128)S(1)} copy(f32[48,20,2]{2,0,1:T(8,128)} %get-tuple-element.41) | data formatting | bytes 15360 | tf_op jit(solution)/shard_map/slice | solution.py:49
  49.9 1.4 %constant_dynamic-update-slice_fusion.4 = bf16[8,64,128]{2,0,1:T(8,128)(2,1)} fusion(bf16[8,64,128]{2,0,1:T(8,128)(2,1)} %constant_dynamic-update-slice_fusion.5, bf16[8,16,128]{2,0,1:T(8,128)(2,1)} %collective-permute-done.5, s32[]{:T(128)S(6)} %select_n.71), kind=kLoop, calls=%fused_computation.81 | loop fusion | bytes 65540 | tf_op jit(solution)/shard_map/dynamic_update_slice | solution.py:33
  52.3 3.2 %collective-permute-done.9 = f32[48,20,2]{0,1,2:T(8,128)S(1)} collective-permute-done((f32[48,20,2]{0,1,2:T(8,128)S(1)}, f32[48,20,2]{0,1,2:T(8,128)S(1)}, u32[]{:S(2)}, u32[]{:S(2)}) %collective-permute-start.9) | collective-permute-done | bytes 7712 | tf_op jit(solution)/shard_map/ppermute | solution.py:48
  56.5 1.6 %maximum_multiply_fusion.1 = f32[48,20,132]{2,0,1:T(8,128)S(1)} fusion(f32[48,20,2]{2,0,1:T(8,128)} %copy.81, f32[48,20,128]{2,0,1:T(8,128)S(1)} %constant_dynamic-update-slice_fusion, f32[48,20,2]{2,0,1:T(8,128)} %copy.80, f32[20]{0:T(128)S(1)} %copy-done.11), kind=kLoop, calls=%fused_computation.25 | loop fusion | flops 380160 | bytes 1013840 | tf_op jit(solution)/shard_map/mul | solution.py:71
  59.2 1.4 %constant_dynamic-update-slice_fusion.3 = bf16[8,64,128]{2,0,1:T(8,128)(2,1)} fusion(bf16[8,64,128]{2,0,1:T(8,128)(2,1)} %constant_dynamic-update-slice_fusion.4, bf16[8,16,128]{2,0,1:T(8,128)(2,1)} %collective-permute-done.6, s32[]{:T(128)S(6)} %select_n.73), kind=kLoop, calls=%fused_computation.80 | loop fusion | bytes 65540 | tf_op jit(solution)/shard_map/dynamic_update_slice | solution.py:25
  60.6 2.3 %gather_fusion = bf16[48,8,128]{2,1,0:T(8,128)(2,1)} fusion(bf16[8,64,128]{2,0,1:T(8,128)(2,1)} %constant_dynamic-update-slice_fusion.3, s32[1024]{0:T(1024)} %pad_clamp_fusion.1), kind=kCustom, calls=%fused_computation.clone | custom fusion | bytes 196800 | tf_op jit(solution)/shard_map/jit(_take)/gather | solution.py:104
  62.9 1.5 %fusion.8 = f32[48,8,128]{2,1,0:T(8,128)S(1)} fusion(bf16[1,48,128,128]{3,2,1,0:T(8,128)(2,1)S(1)} %copy-done, bf16[48,8,128]{2,1,0:T(8,128)(2,1)} %gather_fusion, f32[48]{0:T(128)S(1)} %copy-done.10, pred[48]{0:T(512)(128)(4,1)S(1)} %copy-done.12), kind=kOutput, calls=%fused_computation.16 | convolution fusion | flops 12681216 | bytes 1868016 | tf_op jit(solution)/shard_map/fpt,pts->pfs/dot_general | solution.py:102
  67.9 1.4 %collective-permute-start.2 = (f32[128,20,2]{0,1,2:T(8,128)S(1)}, f32[128,20,2]{0,1,2:T(8,128)S(1)}, u32[]{:S(2)}, u32[]{:S(2)}) collective-permute-start(f32[128,20,2]{0,1,2:T(8,128)S(1)} %get-tuple-element.37), channel_id=1, source_target_pairs={{0,1},{1,2},{2,3},{3,0},{4,5},{5,6},{6,7},{7,4},{8,9},{9,10},{10,1... | collective-permute-start | bytes 61448 | tf_op jit(solution)/shard_map/ppermute | solution.py:48
  71.2 2.5 %collective-permute-done.2 = f32[128,20,2]{0,1,2:T(8,128)S(1)} collective-permute-done((f32[128,20,2]{0,1,2:T(8,128)S(1)}, f32[128,20,2]{0,1,2:T(8,128)S(1)}, u32[]{:S(2)}, u32[]{:S(2)}) %collective-permute-start.2) | collective-permute-done | bytes 20512 | tf_op jit(solution)/shard_map/ppermute | solution.py:48
  74.8 11.9 %reduce-scatter.2.cloned.1.call-done = f32[32,1024]{1,0:T(8,128)} async-done(((f32[128,1024]{1,0:T(8,128)}), f32[32,1024]{1,0:T(8,128)}) %reduce-scatter.2.cloned.1.call-update) | async-done | bytes 131088 | tf_op jit(solution)/shard_map/reduce_scatter | solution.py:129
  87.6 1.3 %copy.74 = f32[16,8,128]{1,2,0:T(8,128)} copy(f32[16,8,128]{2,1,0:T(8,128)S(1)} %bitcast.54) | data formatting | bytes 131072 | tf_op jit(solution)/shard_map/reshape | solution.py:143
  88.9 2.3 %slice_add_fusion.3 = f32[8,16,128]{0,2,1:T(8,128)} fusion(f32[128,16,128]{0,2,1:T(8,128)S(1)} %fusion.16, f32[16,8,128]{1,2,0:T(8,128)} %copy.74), kind=kLoop, calls=%fused_computation.18 | loop fusion | flops 16384 | bytes 196608 | tf_op jit(solution)/shard_map/add | solution.py:149
  91.2 5.1 %scatter-add.6 = f32[128,16,128]{0,2,1:T(8,128)S(1)} dynamic-update-slice(f32[128,16,128]{0,2,1:T(8,128)S(1)} %fusion.16, f32[8,16,128]{0,2,1:T(8,128)} %slice_add_fusion.3, s32[]{:T(128)} %constant.139.clone.1, s32[]{:T(128)} %constant.139.clone.1, s32[]{:T(128)} %constant.139.clone.1) | dynamic-update-slice | bytes 131076 | tf_op jit(solution)/shard_map/scatter-add | solution.py:149
  96.4 1.4 %copy.82 = f32[128,16,128]{2,1,0:T(8,128)} copy(f32[128,16,128]{0,2,1:T(8,128)S(1)} %scatter-add.6) | data formatting | bytes 2097152
  (95 shorter events, 21.2 us)
Async XLA Ops:
  7.2 31.5 %copy-start = (bf16[1,48,128,128]{3,2,1,0:T(8,128)(2,1)S(1)}, bf16[1,48,128,128]{3,2,1,0:T(8,128)(2,1)}, u32[]{:S(2)}) copy-start(bf16[1,48,128,128]{3,2,1,0:T(8,128)(2,1)} %param.20) | copy-start | bytes 4718596
  7.2 79.5 %reduce-scatter.2.cloned.1.call-start = ((), (), s32[]{:S(2)}) async-start(), calls=%async_computation.1 | async-start | bytes 655360 | tf_op jit(solution)/shard_map/reduce_scatter | solution.py:129
  8.9 10.1 %copy-start.2 = (f32[48,16,128]{2,1,0:T(8,128)S(1)}, f32[48,16,128]{2,1,0:T(8,128)}, u32[]{:S(2)}) copy-start(f32[48,16,128]{2,1,0:T(8,128)} %param.16) | copy-start | bytes 1179652
  9.5 10.4 %copy-start.17 = (s32[1,48]{1,0:T(1,128)S(1)}, s32[1,48]{1,0:T(1,128)}, u32[]{:S(2)}) copy-start(s32[1,48]{1,0:T(1,128)} %param.21) | copy-start | bytes 580
  9.5 11.0 %copy-start.15 = (s32[1,48]{1,0:T(1,128)S(1)}, s32[1,48]{1,0:T(1,128)}, u32[]{:S(2)}) copy-start(s32[1,48]{1,0:T(1,128)} %param.22) | copy-start | bytes 580
  9.5 12.8 %copy-start.16 = (s32[16,1]{0,1:T(1,128)S(1)}, s32[16,1]{0,1:T(1,128)}, u32[]{:S(2)}) copy-start(s32[16,1]{0,1:T(1,128)} %param.19) | copy-start | bytes 196
  9.5 31.3 %collective-permute-start.4 = (bf16[8,16,128]{2,0,1:T(8,128)(2,1)}, bf16[8,16,128]{2,0,1:T(8,128)(2,1)}, u32[]{:S(2)}, u32[]{:S(2)}) collective-permute-start(bf16[8,16,128]{2,0,1:T(8,128)(2,1)} %get-tuple-element.36), channel_id=1, source_target_pairs={{0,1},{1,2},{2,3},{3,0},{4,5},{5,6},{6,7},{7,4},{8,9},{9,10},{10,1... | collective-permute-start | bytes 98312 | tf_op jit(solution)/shard_map/ppermute | solution.py:24
  12.6 37.2 %collective-permute-start.5 = (bf16[8,16,128]{2,0,1:T(8,128)(2,1)}, bf16[8,16,128]{2,0,1:T(8,128)(2,1)}, u32[]{:S(2)}, u32[]{:S(2)}) collective-permute-start(bf16[8,16,128]{2,0,1:T(8,128)(2,1)} %get-tuple-element.36), channel_id=1, source_target_pairs={{0,3},{1,0},{2,1},{3,2},{4,7},{5,4},{6,5},{7,6},{8,11},{9,8},{10,9... | collective-permute-start | bytes 98312 | tf_op jit(solution)/shard_map/ppermute | solution.py:32
  17.3 48.7 %collective-permute-start.1 = (f32[128,2,128]{0,1,2:T(2,128)}, f32[128,2,128]{0,1,2:T(2,128)}, u32[]{:S(2)}, u32[]{:S(2)}) collective-permute-start(f32[128,2,128]{0,1,2:T(2,128)} %get-tuple-element.40), channel_id=1, source_target_pairs={{4,0},{8,4},{12,8},{16,12},{20,16},{24,20},{28,24},{0,28},{5,1},{9... | collective-permute-start | bytes 393224 | tf_op jit(solution)/shard_map/ppermute | solution.py:51
  19.0 47.1 %collective-permute-start = (f32[128,2,128]{0,1,2:T(2,128)}, f32[128,2,128]{0,1,2:T(2,128)}, u32[]{:S(2)}, u32[]{:S(2)}) collective-permute-start(f32[128,2,128]{0,1,2:T(2,128)} %get-tuple-element.39), channel_id=1, source_target_pairs={{0,4},{4,8},{8,12},{12,16},{16,20},{20,24},{24,28},{28,0},{1,5},{5... | collective-permute-start | bytes 393224 | tf_op jit(solution)/shard_map/ppermute | solution.py:48
  19.7 22.5 %collective-permute-start.7 = (f32[48,2,128]{2,0,1:T(8,128)S(1)}, f32[48,2,128]{2,0,1:T(8,128)S(1)}, u32[]{:S(2)}, u32[]{:S(2)}) collective-permute-start(f32[48,2,128]{2,0,1:T(8,128)S(1)} %get-tuple-element.44), channel_id=1, source_target_pairs={{0,4},{4,8},{8,12},{12,16},{16,20},{20,24},{24,28},{28,0},{1,5},{5... | collective-permute-start | bytes 147464 | tf_op jit(solution)/shard_map/ppermute | solution.py:48
  21.7 20.5 %copy-start.9 = (f32[48]{0:T(128)}, f32[48]{0:T(128)S(1)}, u32[]{:S(2)}) copy-start(f32[48]{0:T(128)S(1)} %compare_convert_fusion) | copy-start | bytes 580
  40.8 2.1 %collective-permute-start.8 = (f32[48,2,128]{2,0,1:T(8,128)}, f32[48,2,128]{2,0,1:T(8,128)S(1)}, u32[]{:S(2)}, u32[]{:S(2)}) collective-permute-start(f32[48,2,128]{2,0,1:T(8,128)} %get-tuple-element.43), channel_id=1, source_target_pairs={{4,0},{8,4},{12,8},{16,12},{20,16},{24,20},{28,24},{0,28},{5,1},{9... | collective-permute-start | bytes 147464 | tf_op jit(solution)/shard_map/ppermute | solution.py:51
  42.2 17.0 %collective-permute-start.6 = (bf16[8,16,128]{2,0,1:T(8,128)(2,1)}, bf16[8,16,128]{2,0,1:T(8,128)(2,1)}, u32[]{:S(2)}, u32[]{:S(2)}) collective-permute-start(bf16[8,16,128]{2,0,1:T(8,128)(2,1)} %collective-permute-done.4), channel_id=1, source_target_pairs={{0,1},{1,2},{2,3},{3,0},{4,5},{5,6},{6,7},{7,4},{8,9},{9,10},{10,1... | collective-permute-start | bytes 98312 | tf_op jit(solution)/shard_map/ppermute | solution.py:24
  44.0 12.5 %copy-start.11 = (f32[20]{0:T(128)S(1)}, f32[20]{0:T(128)}, u32[]{:S(2)}) copy-start(f32[20]{0:T(128)} %not_convert_fusion.1) | copy-start | bytes 244
  45.2 6.0 %collective-permute-start.10 = (f32[48,20,2]{0,1,2:T(8,128)S(1)}, f32[48,20,2]{0,1,2:T(8,128)S(1)}, u32[]{:S(2)}, u32[]{:S(2)}) collective-permute-start(f32[48,20,2]{0,1,2:T(8,128)S(1)} %copy.79), channel_id=1, source_target_pairs={{1,0},{2,1},{3,2},{0,3},{5,4},{6,5},{7,6},{4,7},{9,8},{10,9},{11,1... | collective-permute-start | bytes 23048 | tf_op jit(solution)/shard_map/ppermute | solution.py:51
  49.8 5.7 %collective-permute-start.9 = (f32[48,20,2]{0,1,2:T(8,128)S(1)}, f32[48,20,2]{0,1,2:T(8,128)S(1)}, u32[]{:S(2)}, u32[]{:S(2)}) collective-permute-start(f32[48,20,2]{0,1,2:T(8,128)S(1)} %copy.78), channel_id=1, source_target_pairs={{0,1},{1,2},{2,3},{3,0},{4,5},{5,6},{6,7},{7,4},{8,9},{9,10},{10,1... | collective-permute-start | bytes 23048 | tf_op jit(solution)/shard_map/ppermute | solution.py:48
  52.3 5.9 %copy-start.4 = (f32[48]{0:T(128)S(1)}, f32[48]{0:T(128)}, u32[]{:S(2)}) copy-start(f32[48]{0:T(128)} %param.18) | copy-start | bytes 580
  52.3 5.9 %copy-start.8 = (f32[18]{0:T(128)S(1)}, f32[18]{0:T(128)}, u32[]{:S(2)}) copy-start(f32[18]{0:T(128)} %not_convert_fusion) | copy-start | bytes 220
  58.2 4.7 %copy-start.10 = (f32[48]{0:T(128)S(1)}, f32[48]{0:T(128)}, u32[]{:S(2)}) copy-start(f32[48]{0:T(128)} %copy-done.9) | copy-start | bytes 580
  58.2 4.7 %copy-start.12 = (pred[48]{0:T(512)(128)(4,1)S(1)}, pred[48]{0:T(512)(128)(4,1)}, u32[]{:S(2)}) copy-start(pred[48]{0:T(512)(128)(4,1)} %compare_and_fusion.1) | copy-start | bytes 148
  59.2 5.2 %copy-start.13 = (s32[48]{0:T(128)S(1)}, s32[48]{0:T(128)}, u32[]{:S(2)}) copy-start(s32[48]{0:T(128)} %fusion.43) | copy-start | bytes 580
  67.3 3.9 %collective-permute-start.3 = (f32[128,20,2]{0,1,2:T(8,128)S(1)}, f32[128,20,2]{0,1,2:T(8,128)S(1)}, u32[]{:S(2)}, u32[]{:S(2)}) collective-permute-start(f32[128,20,2]{0,1,2:T(8,128)S(1)} %get-tuple-element.38), channel_id=1, source_target_pairs={{1,0},{2,1},{3,2},{0,3},{5,4},{6,5},{7,6},{4,7},{9,8},{10,9},{11,1... | collective-permute-start | bytes 61448 | tf_op jit(solution)/shard_map/ppermute | solution.py:51
  67.9 5.7 %collective-permute-start.2 = (f32[128,20,2]{0,1,2:T(8,128)S(1)}, f32[128,20,2]{0,1,2:T(8,128)S(1)}, u32[]{:S(2)}, u32[]{:S(2)}) collective-permute-start(f32[128,20,2]{0,1,2:T(8,128)S(1)} %get-tuple-element.37), channel_id=1, source_target_pairs={{0,1},{1,2},{2,3},{3,0},{4,5},{5,6},{6,7},{7,4},{8,9},{9,10},{10,1... | collective-permute-start | bytes 61448 | tf_op jit(solution)/shard_map/ppermute | solution.py:48
  (6 other events, 12.2 us)
Sparse Core Ops, SparseCore 0:
  66.1 20.4 reduce-scatter.1
